TPU v7x, 32 devices: a whole 2x2x4 slice. The times are simulated.
32 devices in a mesh: row: 4 (over y, x), col: 8 (over z, core).
Axes of the slice: x: 2, y: 2, z: 4, core: 2. Of those that a mesh axis runs over, the one named last changes fastest.
Arguments:
- scalar_field: float32 [256, 256, 1024], P('col', 'row'), may hold values from -1.2 to 1.2
- reaction: float32 [256, 256, 1024], P('col', 'row'), may hold values from 0.5 to 4
- x_faces: float32 [1024], replicated, may hold values from 0.5 to 4
- y_faces: float32 [256], replicated, may hold values from 0.5 to 4
- z_faces: float32 [256], replicated, may hold values from 0.5 to 4
- x_inverse: float32 [8, 128, 128], replicated, may hold values from 0 to 1, as said below
- y_inverse: float32 [2, 128, 128], replicated, may hold values from 0 to 1, as said below
- z_inverse: float32 [2, 128, 128], replicated, may hold values from 0 to 1, as said below
Outputs:
- advanced: float32 [256, 256, 1024], P('col', 'row')
Inputs may be any that keep to these rules, and one draw needn't show every extreme that they name: x_inverse[c] is, up to float32 rounding, the inverse of the block of rows and columns c * 128 to (c + 1) * 128 - 1 of the matrix I - 500 A_x along one x line. y_inverse[c] is, up to float32 rounding, the inverse of the block of rows and columns c * 128 to (c + 1) * 128 - 1 of the matrix I - 500 A_y along one y line. z_inverse[c] is, up to float32 rounding, the inverse of the block of rows and columns c * 128 to (c + 1) * 128 - 1 of the matrix I - 500 A_z along one z line.
All inputs are finite; a program needn't handle non-finite values.
Results may differ from a plain program's by a relative error of at most 0.0003.
Values sent between devices are 32-bit elements; how exact they have to be, the bound alone decides.
A program may use at most 128 MiB of HBM per device.

v0:
```python
import jax
import jax.numpy as jnp
from jax import lax
from jax.sharding import PartitionSpec as P

implicit_weight = 0.5
time_step = 1000.0


def with_halo(shard, sides, width):
    for axis, dim in sides:
        size, length = (lax.axis_size(axis), shard.shape[dim])
        up = [(i, (i + 1) % size) for i in range(size - 1)]
        down = [(j, i) for i, j in up]
        last = lax.slice_in_dim(shard, length - width, length, axis=dim)
        leading = lax.slice_in_dim(shard, 0, width, axis=dim)
        before = lax.ppermute(last, axis, up)
        after = lax.ppermute(leading, axis, down)
        shard = jnp.concatenate([before, shard, after], axis=dim)
    return shard


def shift_lower(values, line_axis):
    length = values.shape[line_axis]
    first_slot = jnp.zeros_like(lax.slice_in_dim(values, 0, 1, axis=line_axis))
    return jnp.concatenate(
        [first_slot, lax.slice_in_dim(values, 0, length - 1, axis=line_axis)], axis=line_axis
    )


def shift_upper(values, line_axis):
    length = values.shape[line_axis]
    last_slot = jnp.zeros_like(lax.slice_in_dim(values, 0, 1, axis=line_axis))
    return jnp.concatenate(
        [lax.slice_in_dim(values, 1, length, axis=line_axis), last_slot], axis=line_axis
    )


def apply_line(values, face_values, line_axis):
    spread = [1, 1, 1]
    spread[line_axis] = values.shape[line_axis]
    face_here = face_values.reshape(spread)
    face_next = jnp.concatenate([face_values[1:], jnp.zeros((1,), face_values.dtype)]).reshape(
        spread
    )
    lower_value = shift_lower(values, line_axis)
    upper_value = shift_upper(values, line_axis)
    return face_next * (upper_value - values) - face_here * (values - lower_value)


def invert_small(matrix):
    order = matrix.shape[0]
    joined = jnp.concatenate([matrix, jnp.eye(order, dtype=matrix.dtype)], axis=1)

    def sweep(step_index, current):
        pivot_row = lax.dynamic_index_in_dim(current, step_index, 0, keepdims=False)
        pivot_row = pivot_row / lax.dynamic_index_in_dim(pivot_row, step_index, 0, keepdims=False)
        pivot_column = lax.dynamic_slice_in_dim(current, step_index, 1, 1)
        current = current - pivot_column * pivot_row[None, :]
        return lax.dynamic_update_index_in_dim(current, pivot_row, step_index, 0)

    joined = lax.fori_loop(0, order, sweep, joined)
    return joined[:, order:]


def reduced_inverse(inverse, coupling_before, coupling_after):
    groups, block_width = (inverse.shape[0], inverse.shape[1])
    order = 2 * groups
    group_index = jnp.arange(groups)
    lead_rows = 2 * group_index
    trail_rows = 2 * group_index + 1
    prev_cols = jnp.maximum(2 * group_index - 1, 0)
    next_cols = jnp.minimum(2 * group_index + 2, order - 1)
    coupled = jnp.zeros((order, order), inverse.dtype)
    coupled = coupled.at[lead_rows, prev_cols].add(coupling_before * inverse[:, 0, 0])
    coupled = coupled.at[lead_rows, next_cols].add(coupling_after * inverse[:, 0, block_width - 1])
    coupled = coupled.at[trail_rows, prev_cols].add(
        coupling_before * inverse[:, block_width - 1, 0]
    )
    coupled = coupled.at[trail_rows, next_cols].add(
        coupling_after * inverse[:, block_width - 1, block_width - 1]
    )
    return invert_small(jnp.eye(order, dtype=inverse.dtype) - coupled)


def line_solve(right_side, inverse, face_values, line_axis):
    groups, block_width = (inverse.shape[0], inverse.shape[1])
    dims_full = right_side.shape
    blocked = right_side.reshape(
        dims_full[:line_axis] + (groups, block_width) + dims_full[line_axis + 1 :]
    )
    others = ["u", "v"]
    source = "".join(others[:line_axis] + ["c", "j"] + others[line_axis:])
    target = "".join(others[:line_axis] + ["c", "i"] + others[line_axis:])
    inside = jnp.einsum(
        "cij," + source + "->" + target, inverse, blocked, precision=lax.Precision.HIGHEST
    )
    leading = lax.index_in_dim(inside, 0, line_axis + 1, keepdims=False)
    trailing = lax.index_in_dim(inside, block_width - 1, line_axis + 1, keepdims=False)
    coupling = implicit_weight * time_step * face_values[block_width::block_width]
    nothing = jnp.zeros((1,), face_values.dtype)
    coupling_before = jnp.concatenate([nothing, coupling])
    coupling_after = jnp.concatenate([coupling, nothing])
    reduced = reduced_inverse(inverse, coupling_before, coupling_after)
    interface = jnp.stack([leading, trailing], axis=line_axis + 1)
    interface = interface.reshape(
        dims_full[:line_axis] + (2 * groups,) + dims_full[line_axis + 1 :]
    )
    end_source = "".join(others[:line_axis] + ["j"] + others[line_axis:])
    end_target = "".join(others[:line_axis] + ["i"] + others[line_axis:])
    solved = jnp.einsum(
        "ij," + end_source + "->" + end_target, reduced, interface, precision=lax.Precision.HIGHEST
    )
    solved = solved.reshape(dims_full[:line_axis] + (groups, 2) + dims_full[line_axis + 1 :])
    first_values = lax.index_in_dim(solved, 0, line_axis + 1, keepdims=False)
    last_values = lax.index_in_dim(solved, 1, line_axis + 1, keepdims=False)
    prev_last = shift_lower(last_values, line_axis)
    next_first = shift_upper(first_values, line_axis)
    spike_shape = [1, 1, 1, 1]
    spike_shape[line_axis] = groups
    spike_shape[line_axis + 1] = block_width
    left_spike = (coupling_before[:, None] * inverse[:, :, 0]).reshape(spike_shape)
    right_spike = (coupling_after[:, None] * inverse[:, :, block_width - 1]).reshape(spike_shape)
    result = (
        inside
        + left_spike * jnp.expand_dims(prev_last, line_axis + 1)
        + right_spike * jnp.expand_dims(next_first, line_axis + 1)
    )
    return result.reshape(dims_full)


def body(scalar_field, reaction, x_faces, y_faces, z_faces, x_inverse, y_inverse, z_inverse):
    z_cells, y_cells, x_cells = scalar_field.shape
    padded = with_halo(scalar_field, (("row", 1), ("col", 0)), 1)
    nothing = jnp.zeros((1,), jnp.float32)
    y_padded = jnp.concatenate([y_faces, nothing])
    z_padded = jnp.concatenate([z_faces, nothing])
    y_start = lax.axis_index("row") * y_cells
    z_start = lax.axis_index("col") * z_cells
    y_here = lax.dynamic_slice_in_dim(y_padded, y_start, y_cells).reshape(1, y_cells, 1)
    y_next = lax.dynamic_slice_in_dim(y_padded, y_start + 1, y_cells).reshape(1, y_cells, 1)
    z_here = lax.dynamic_slice_in_dim(z_padded, z_start, z_cells).reshape(z_cells, 1, 1)
    z_next = lax.dynamic_slice_in_dim(z_padded, z_start + 1, z_cells).reshape(z_cells, 1, 1)
    y_term = y_next * (padded[1:-1, 2:, :] - scalar_field) - y_here * (
        scalar_field - padded[1:-1, :-2, :]
    )
    z_term = z_next * (padded[2:, 1:-1, :] - scalar_field) - z_here * (
        scalar_field - padded[:-2, 1:-1, :]
    )
    x_term = apply_line(scalar_field, x_faces, 2)
    source = reaction * scalar_field * (1.0 - scalar_field * scalar_field)
    change = time_step * (x_term + y_term + z_term + source)
    first_section = line_solve(change, x_inverse, x_faces, 2)
    section_y = lax.all_to_all(first_section, "row", split_axis=2, concat_axis=1, tiled=True)
    second_section = line_solve(section_y, y_inverse, y_faces, 1)
    section_z = lax.all_to_all(second_section, "col", split_axis=1, concat_axis=0, tiled=True)
    total_change = line_solve(section_z, z_inverse, z_faces, 0)
    returned = lax.all_to_all(
        lax.all_to_all(total_change, "col", split_axis=0, concat_axis=1, tiled=True),
        "row",
        split_axis=1,
        concat_axis=2,
        tiled=True,
    )
    return scalar_field + returned


def solution(mesh):
    in_specs = (P("col", "row", None), P("col", "row", None), P(), P(), P(), P(), P(), P())
    out_specs = P("col", "row", None)
    return jax.shard_map(body, mesh=mesh, in_specs=in_specs, out_specs=out_specs, check_vma=False)
```

profile of v0, /device:TPU:0, one launch (start us, length us, event | category | flops | bytes accessed | tf_op | source)
XLA Modules:
  0.0 899.9 jit_solution(2791366461174702454)
XLA Ops:
  0.0 1.8 fusion.73
  1.8 1.3 collective-permute-start
  3.1 5.5 collective-permute-start.1
  8.7 13.3 %fusion.72 = (f32[32,64,1023]{2,1,0:T(8,128)}, f32[32,64,1023]{2,1,0:T(8,128)}) fusion(f32[32,64,1024]{2,1,0:T(8,128)} %param.14), kind=kLoop, calls=%fused_computation.182 | loop fusion | bytes 33521664 | tf_op jit(solution)/shard_map/slice | solution.py:35
  22.7 0.9 scatter_fusion
  23.6 0.9 scatter_fusion.1
  24.4 0.9 scatter_fusion.2
  25.3 0.9 scatter_fusion.3
  26.2 32.5 %while.39 = (s32[]{:T(128)}, f32[16,32]{1,0:T(8,128)S(1)}, s32[]{:T(128)}, s32[]{:T(128)}, s32[]{:T(128)}, /*index=5*/s32[]{:T(128)}) while((s32[]{:T(128)}, f32[16,32]{1,0:T(8,128)S(1)}, s32[]{:T(128)}, s32[]{:T(128)}, s32[]{:T(128)}, /*index=5*/s32[]{:T(128)}) %tuple.111), condition=%wide.region_5.6_spmd, body=%wide.region_4.5_spmd.sunk | while | flops 1092 | bytes 5321 | solution.py:62
  59.3 1.1 pad_maximum_fusion.11
  60.4 1.3 collective-permute-start.2
  61.7 3.2 collective-permute-start.3
  66.0 28.5 %fusion.22 = f32[32,64,8,128]{3,1,0,2:T(8,128)S(1)} fusion(f32[8,128,128]{2,1,0:T(8,128)S(1)} %copy-done.2, f32[32,64,1024]{2,1,0:T(8,128)} %param.14, f32[1,66,1024]{2,1,0:T(8,128)S(1)} %collective-permute-done.3, f32[32,1,1024]{2,1,0:T(1,128)S(1)} %copy.140, f32[32,1,1024]{2,1,0:T(1,128)S(1)} %copy.142, f32[1,66,1024]{2,1,0:T(8,128)S(1)} %collective-permute-done.2, ...), kind=kOutput, calls=%fused_computation.55 | convolution fusion | flops 3286237184 | bytes 43262720 | tf_op jit(solution)/shard_map/cij,uvcj->uvci/dot_general | solution.py:95
  94.4 7.9 fusion.71
  102.9 11.9 %pad_maximum_fusion.8 = f32[32,64,8,2]{3,1,0,2:T(8,128)} fusion(f32[32,64,8,1]{3,1,0,2:T(8,128)} %get-tuple-element.190, f32[32,64,8,1]{3,1,0,2:T(8,128)} %get-tuple-element.189), kind=kLoop, calls=%fused_computation.47 | loop fusion | flops 32768 | bytes 262144 | tf_op jit(solution)/shard_map/stack | solution.py:105
  114.8 5.4 copy.147
  120.9 10.5 %multiply_add_fusion.2 = f32[32,64,8,128]{3,1,0,2:T(8,128)} fusion(f32[32,64,8,128]{3,1,0,2:T(8,128)} %copy-done, f32[32,64,8]{1,0,2:T(8,128)S(1)} %concatenate.122.clone, f32[8,128]{1,0:T(8,128)S(1)} %get-tuple-element.229, f32[32,64,8]{1,0,2:T(8,128)S(1)} %concatenate.121.clone, f32[8,128]{1,0:T(8,128)S(1)} %get-tuple-element.230), kind=kLoop, calls=%fused_computation.54 | loop fusion | flops 8388608 | bytes 16916480 | tf_op jit(solution)/shard_map/add | solution.py:125
  131.4 16.2 %copy.183 = f32[32,64,8,128]{1,0,3,2:T(8,128)} copy(f32[32,64,8,128]{3,1,0,2:T(8,128)} %multiply_add_fusion.2) | data formatting | bytes 16777216 | tf_op jit(solution)/shard_map/reshape | solution.py:129
  147.6 14.7 %reshape.391 = f32[4,1,524288]{2,1,0:T(1,128)} reshape(f32[1024,32,64]{2,1,0:T(8,128)} %bitcast.128) | data formatting | bytes 16777216
  162.3 5.8 all-to-all-start
  170.6 0.6 scatter_fusion.8
  171.5 0.6 scatter_fusion.4
  172.3 0.6 scatter_fusion.9
  173.0 0.6 scatter_fusion.5
  173.6 0.6 scatter_fusion.10
  174.2 0.6 scatter_fusion.6
  174.9 0.6 scatter_fusion.11
  175.5 0.6 scatter_fusion.7
  176.8 8.8 while.40
  176.8 0.6 dynamic_slice.112
  177.4 0.6 dynamic-slice_divide_fusion.7
  178.0 0.6 fusion.88
  178.9 0.6 dynamic_slice.112
  179.5 0.6 dynamic-slice_divide_fusion.7
  180.2 0.6 fusion.88
  181.1 0.6 dynamic_slice.112
  181.7 0.6 dynamic-slice_divide_fusion.7
  182.4 0.6 fusion.88
  183.9 0.6 dynamic-slice_divide_fusion.7
  184.6 0.6 fusion.88
  185.5 75.3 %all-to-all-done = f32[4,1,524288]{2,1,0:T(1,128)} async-done(((f32[4,1,524288]{2,1,0:T(1,128)}), f32[4,1,524288]{2,1,0:T(1,128)}, u32[]{:S(2)}, u32[]{:S(2)}) %all-to-all-start) | async-done | bytes 8388640 | tf_op jit(solution)/shard_map/all_to_all | solution.py:154
  261.3 28.3 %reduce.38 = f32[4,524288]{1,0:T(4,128)} reduce(f32[4,1,524288]{2,1,0:T(1,128)} %all-to-all-done, f32[]{:T(128)} %broadcast.1002), dimensions={1}, to_apply=%all_to_all.48.reduce_sub_computation | reduce | bytes 16777220 | tf_op jit(solution)/shard_map/all_to_all | solution.py:154
  289.7 16.8 %reshape.392 = f32[1024,32,64]{2,1,0:T(8,128)} reshape(f32[4,524288]{1,0:T(4,128)} %reduce.38) | data formatting | bytes 16777216
  306.4 13.0 %copy.184 = f32[32,64,4,256]{3,2,1,0:T(4,128)} copy(f32[32,64,4,256]{1,0,3,2:T(8,128)} %bitcast.129) | data formatting | bytes 16777216 | tf_op jit(solution)/shard_map/all_to_all | solution.py:154
  319.4 5.0 copy.156
  324.4 8.6 fusion.25
  333.1 3.4 copy-done.1
  337.5 5.4 multiply_add_fusion.1
  342.8 1.4 copy.162
  344.2 8.3 copy.163
  352.5 8.6 all-to-all-start.1
  361.1 8.1 while.41
  369.7 175.4 %all-to-all-done.1 = f32[32,256,256]{2,0,1:T(8,128)} async-done(((f32[32,256,256]{2,0,1:T(8,128)}), f32[32,256,256]{2,0,1:T(8,128)}, u32[]{:S(2)}, u32[]{:S(2)}) %all-to-all-start.1) | async-done | bytes 8388640 | tf_op jit(solution)/shard_map/all_to_all | solution.py:156
  545.1 8.2 copy.165
  553.3 13.4 %fusion.28 = f32[2,128,32,256]{3,1,2,0:T(8,128)S(1)} fusion(f32[2,128,32,256]{3,2,1,0:T(8,128)S(1)} %bitcast.133, f32[2,128,128]{2,1,0:T(8,128)S(1)} %copy-done.4), kind=kOutput, calls=%fused_computation.57 | convolution fusion | flops 3221225472 | bytes 16908288 | tf_op jit(solution)/shard_map/cij,cjuv->ciuv/dot_general | solution.py:95
  567.6 2.3 multiply_add_fusion
  569.9 5.1 copy.171
  574.9 186.4 %all_to_all.66 = f32[256,32,256]{2,1,0:T(8,128)S(1)} all-to-all(f32[256,32,256]{2,1,0:T(8,128)S(1)} %bitcast.134), channel_id=1, replica_groups=mesh['row'=4,'col'=8] {'col'}, dimensions={0} | all-to-all | bytes 16777216 | tf_op jit(solution)/shard_map/all_to_all | solution.py:159
  761.4 1.7 copy.172
  763.0 4.9 copy.173
  767.9 96.7 %all_to_all.67 = f32[32,256,256]{2,0,1:T(8,128)} all-to-all(f32[32,256,256]{2,0,1:T(8,128)S(1)} %copy.173), channel_id=1, replica_groups=mesh['row'=4,'col'=8] {'row'}, dimensions={1} | all-to-all | bytes 16777216 | tf_op jit(solution)/shard_map/all_to_all | solution.py:158
  864.6 12.2 %copy.175 = f32[32,64,4,256]{3,2,1,0:T(4,128)} copy(f32[32,64,4,256]{3,0,1,2:T(8,128)} %bitcast.137) | data formatting | bytes 16777216 | tf_op jit(solution)/shard_map/all_to_all | solution.py:158
  876.8 10.7 %all_to_all.61 = f32[32,64,1024]{2,1,0:T(8,128)} reshape(f32[32,64,4,256]{3,2,1,0:T(4,128)} %copy.175) | data formatting | bytes 16777216 | tf_op jit(solution)/shard_map/all_to_all | solution.py:158
  887.5 12.1 %add.391 = f32[32,64,1024]{2,1,0:T(8,128)} add(f32[32,64,1024]{2,1,0:T(8,128)} %param.14, f32[32,64,1024]{2,1,0:T(8,128)} %all_to_all.61) | non-fusion elementwise | flops 2097152 | bytes 25165824 | tf_op jit(solution)/shard_map/add | solution.py:165
  (234 shorter events, 50.3 us)
Async XLA Ops:
  1.8 57.2 %collective-permute-start = (f32[32,1,1024]{2,0,1:T(8,128)S(1)}, f32[32,1,1024]{2,0,1:T(8,128)S(1)}, u32[]{:S(2)}, u32[]{:S(2)}) collective-permute-start(f32[32,1,1024]{2,0,1:T(8,128)S(1)} %copy.188), channel_id=1, source_target_pairs={{8,0},{16,8},{24,16},{9,1},{17,9},{25,17},{10,2},{18,10},{26,18},{... | collective-permute-start | bytes 393224 | tf_op jit(solution)/shard_map/ppermute | solution.py:18
  3.1 56.0 %collective-permute-start.1 = (f32[32,1,1024]{2,0,1:T(8,128)S(1)}, f32[32,1,1024]{2,0,1:T(8,128)S(1)}, u32[]{:S(2)}, u32[]{:S(2)}) collective-permute-start(f32[32,1,1024]{2,0,1:T(8,128)S(1)} %copy.189), channel_id=1, source_target_pairs={{0,8},{8,16},{16,24},{1,9},{9,17},{17,25},{2,10},{10,18},{18,26},{... | collective-permute-start | bytes 393224 | tf_op jit(solution)/shard_map/ppermute | solution.py:17
  8.7 13.4 %copy-start.2 = (f32[8,128,128]{2,1,0:T(8,128)S(1)}, f32[8,128,128]{2,1,0:T(8,128)}, u32[]{:S(2)}) copy-start(f32[8,128,128]{2,1,0:T(8,128)} %param.19) | copy-start | bytes 1572868
  8.7 13.8 %copy-start.5 = (f32[1024]{0:T(1024)S(1)}, f32[1024]{0:T(1024)}, u32[]{:S(2)}) copy-start(f32[1024]{0:T(1024)} %param.16) | copy-start | bytes 12292
  8.7 50.1 %copy-start.6 = (f32[256]{0:T(256)S(1)}, f32[256]{0:T(256)}, u32[]{:S(2)}) copy-start(f32[256]{0:T(256)} %param.18) | copy-start | bytes 3076
  8.7 50.1 %copy-start.7 = (f32[256]{0:T(256)S(1)}, f32[256]{0:T(256)}, u32[]{:S(2)}) copy-start(f32[256]{0:T(256)} %param.17) | copy-start | bytes 3076
  60.4 5.1 collective-permute-start.2
  61.7 4.2 collective-permute-start.3
  94.4 8.4 copy-start
  162.3 8.1 copy-start.4
  162.3 9.0 copy-start.3
  162.3 98.6 %all-to-all-start = ((f32[4,1,524288]{2,1,0:T(1,128)}), f32[4,1,524288]{2,1,0:T(1,128)}, u32[]{:S(2)}, u32[]{:S(2)}) async-start(f32[4,1,524288]{2,1,0:T(1,128)} %reshape.391), calls=%async_computation | async-start | bytes 16777216 | tf_op jit(solution)/shard_map/all_to_all | solution.py:154
  333.1 3.4 copy-start.1
  352.5 192.6 %all-to-all-start.1 = ((f32[32,256,256]{2,0,1:T(8,128)}), f32[32,256,256]{2,0,1:T(8,128)}, u32[]{:S(2)}, u32[]{:S(2)}) async-start(f32[32,256,256]{2,0,1:T(8,128)} %copy.163), calls=%async_computation.1 | async-start | bytes 16777216 | tf_op jit(solution)/shard_map/all_to_all | solution.py:156
where the time goes:
time: 905 us; the launch traced here: 900 us
  blocking collectives  283 us (31%)
  waiting for transfers between devices  251 us (28%)
  local copies, waits for them, and re-layouts  174 us (19%)
  other arithmetic  112 us (12%)
  matrix products  51.9 us (6%)
  starting transfers between devices  25.8 us (3%)
    all_to_all x1, blocking collectives, body(): lax.all_to_all(total_change, 'col', split_axis=0, concat_axis=1, tiled=True)  186 us
    all_to_all x1, waiting for transfers between devices, body(): lax.all_to_all(second_section, 'col', split_axis=1, concat_axis=0, tiled=...  175 us
    all_to_all x1, blocking collectives, body(): lax.all_to_all(lax.all_to_all(total_change, 'col', split_axis=0, concat_a...  96.7 us
    all_to_all x1, waiting for transfers between devices, body(): lax.all_to_all(first_section, 'row', split_axis=2, concat_axis=1, tiled=T...  75.3 us
    dot_general x3, matrix products, line_solve(): jnp.einsum('cij,' + source + '->' + target, inverse, blocked, precision=l...  50.5 us
    unnamed x28, local copies, waits for them, and re-layouts  35.9 us
    all_to_all x1, other arithmetic, body(): lax.all_to_all(first_section, 'row', split_axis=2, concat_axis=1, tiled=T...  28.3 us
    reshape x2, local copies, waits for them, and re-layouts, line_solve(): return result.reshape(dims_full)  24.5 us
  transfers between devices with their start and end apart: 6, of which 3 were waited for; matrix products, arithmetic and copies ran while one was open for 8% of the time, Pallas kernels for 0%

commit v1 on v0

--- a/solution.py
+++ b/solution.py
@@ -130,6 +130,18 @@
 
 
 def body(scalar_field, reaction, x_faces, y_faces, z_faces, x_inverse, y_inverse, z_inverse):
+
+    def make_spots(load, mesh_ax):
+        return jnp.concatenate(
+            lax.all_to_all(
+                jnp.stack(jnp.split(load, lax.axis_size(mesh_ax), 2), 0),
+                axis_name=mesh_ax,
+                split_axis=0,
+                concat_axis=0,
+            ),
+            1,
+        )
+
     z_cells, y_cells, x_cells = scalar_field.shape
     padded = with_halo(scalar_field, (("row", 1), ("col", 0)), 1)
     nothing = jnp.zeros((1,), jnp.float32)
@@ -151,7 +163,7 @@
     source = reaction * scalar_field * (1.0 - scalar_field * scalar_field)
     change = time_step * (x_term + y_term + z_term + source)
     first_section = line_solve(change, x_inverse, x_faces, 2)
-    section_y = lax.all_to_all(first_section, "row", split_axis=2, concat_axis=1, tiled=True)
+    section_y = make_spots(first_section, "row")
     second_section = line_solve(section_y, y_inverse, y_faces, 1)
     section_z = lax.all_to_all(second_section, "col", split_axis=1, concat_axis=0, tiled=True)
     total_change = line_solve(section_z, z_inverse, z_faces, 0)

time: 905 us -> 817 us (0.903)
  local copies, waits for them, and re-layouts: 174 us -> 113 us
  other arithmetic: 112 us -> 84.7 us
    unnamed x28 -> x26, local copies, waits for them, and re-layouts: 35.9 us -> 4.47 us
    all_to_all x1 -> x0, other arithmetic: 28.3 us -> none  [body(): lax.all_to_all(first_section, 'row', split_axis=2, concat_axis=1, tiled=T...]
    all_to_all x3 -> x0, local copies, waits for them, and re-layouts: 18.5 us -> none  [body(): lax.all_to_all(first_section, 'row', split_axis=2, concat_axis=1, tiled=T...]
    reshape x2 -> x1, local copies, waits for them, and re-layouts: 24.5 us -> 8.66 us  [line_solve(): return result.reshape(dims_full)]
    add x3 -> x2, other arithmetic: 18.2 us -> 7.66 us  [line_solve(): inside + left_spike * jnp.expand_dims(prev_last, line_axis + 1)]
  transfers between devices with their start and end apart: 6 -> 6, of which waited for: 3 -> 2; matrix products, arithmetic and copies ran while one was open for 8% -> 9% of each run, Pallas kernels for 0% -> 0%
where the time goes in v1:
time: 817 us; the launch traced here: 812 us
  blocking collectives  283 us (35%)
  waiting for transfers between devices  251 us (31%)
  local copies, waits for them, and re-layouts  113 us (14%)
  other arithmetic  84.7 us (10%)
  matrix products  51.9 us (6%)
  starting transfers between devices  26.1 us (3%)
    all_to_all x1, blocking collectives, body(): lax.all_to_all(total_change, 'col', split_axis=0, concat_axis=1, tiled=True)  186 us
    all_to_all x1, waiting for transfers between devices, body(): lax.all_to_all(second_section, 'col', split_axis=1, concat_axis=0, tiled=...  175 us
    all_to_all x1, blocking collectives, body(): lax.all_to_all(lax.all_to_all(total_change, 'col', split_axis=0, concat_a...  96.7 us
    all_to_all x1, waiting for transfers between devices, make_spots(): lax.all_to_all(jnp.stack(jnp.split(load, lax.axis_size(mesh_ax), 2), 0),...  75.2 us
    dot_general x3, matrix products, line_solve(): jnp.einsum('cij,' + source + '->' + target, inverse, blocked, precision=l...  50.5 us
    all_to_all x2, local copies, waits for them, and re-layouts, body(): lax.all_to_all(lax.all_to_all(total_change, 'col', split_axis=0, concat_a...  22.9 us
  transfers between devices with their start and end apart: 6, of which 2 were waited for; matrix products, arithmetic and copies ran while one was open for 9% of the time, Pallas kernels for 0%

profile of v1, /device:TPU:0, one launch (start us, length us, event | category | flops | bytes accessed | tf_op | source)
XLA Modules:
  0.0 812.1 jit_solution(12161690091487228929)
XLA Ops:
  0.0 1.8 fusion.73
  1.8 1.3 collective-permute-start
  3.1 5.5 collective-permute-start.1
  8.7 13.3 %fusion.72 = (f32[32,64,1023]{2,1,0:T(8,128)}, f32[32,64,1023]{2,1,0:T(8,128)}) fusion(f32[32,64,1024]{2,1,0:T(8,128)} %param.14), kind=kLoop, calls=%fused_computation.188 | loop fusion | bytes 33521664 | tf_op jit(solution)/shard_map/slice | solution.py:35
  22.7 0.9 scatter_fusion
  23.6 0.9 scatter_fusion.1
  24.4 0.9 scatter_fusion.2
  25.3 0.9 scatter_fusion.3
  26.2 32.5 %while.39 = (s32[]{:T(128)}, f32[16,32]{1,0:T(8,128)S(1)}, s32[]{:T(128)}, s32[]{:T(128)}, s32[]{:T(128)}, /*index=5*/s32[]{:T(128)}) while((s32[]{:T(128)}, f32[16,32]{1,0:T(8,128)S(1)}, s32[]{:T(128)}, s32[]{:T(128)}, s32[]{:T(128)}, /*index=5*/s32[]{:T(128)}) %tuple.114), condition=%wide.region_5.6_spmd, body=%wide.region_4.5_spmd.sunk | while | flops 1092 | bytes 5321 | solution.py:62
  27.4 0.6 fusion.87
  29.4 0.6 fusion.87
  59.3 1.1 pad_maximum_fusion.12
  60.4 1.3 collective-permute-start.2
  61.7 3.6 collective-permute-start.3
  66.0 28.5 %fusion.22 = f32[32,64,8,128]{3,1,0,2:T(8,128)S(1)} fusion(f32[8,128,128]{2,1,0:T(8,128)S(1)} %copy-done.2, f32[32,64,1024]{2,1,0:T(8,128)} %param.14, f32[1,66,1024]{2,1,0:T(8,128)S(1)} %collective-permute-done.3, f32[32,1,1024]{2,1,0:T(1,128)S(1)} %copy.138, f32[32,1,1024]{2,1,0:T(1,128)S(1)} %copy.140, f32[1,66,1024]{2,1,0:T(8,128)S(1)} %collective-permute-done.2, ...), kind=kOutput, calls=%fused_computation.57 | convolution fusion | flops 3286237184 | bytes 43262720 | tf_op jit(solution)/shard_map/cij,uvcj->uvci/dot_general | solution.py:95
  94.4 7.9 fusion.71
  102.9 11.9 %pad_maximum_fusion.8 = f32[32,64,8,2]{3,1,0,2:T(8,128)} fusion(f32[32,64,8,1]{3,1,0,2:T(8,128)} %get-tuple-element.194, f32[32,64,8,1]{3,1,0,2:T(8,128)} %get-tuple-element.193), kind=kLoop, calls=%fused_computation.48 | loop fusion | flops 32768 | bytes 262144 | tf_op jit(solution)/shard_map/stack | solution.py:105
  114.8 5.4 copy.145
  120.9 8.2 %copy_bitcast_fusion = f32[32,64,1024]{2,1,0:T(8,128)S(1)} fusion(f32[32,64,8,128]{3,1,0,2:T(8,128)} %copy-done, f32[32,64,8]{1,0,2:T(8,128)S(1)} %concatenate.122.clone, f32[8,128]{1,0:T(8,128)S(1)} %get-tuple-element.233, f32[32,64,8]{1,0,2:T(8,128)S(1)} %concatenate.121.clone, f32[8,128]{1,0:T(8,128)S(1)} %get-tuple-element.234), kind=kLoop, calls=%fused_computation.21 | loop fusion | flops 8388608 | bytes 16916480 | tf_op jit(solution)/shard_map/reshape | solution.py:129
  129.1 1.3 slice_bitcast_fusion.3
  130.4 3.7 pad_maximum_fusion.9
  134.0 5.8 all-to-all-start
  142.4 0.6 scatter_fusion.8
  143.3 0.6 scatter_fusion.4
  144.0 0.6 scatter_fusion.9
  144.7 0.6 scatter_fusion.5
  145.3 0.6 scatter_fusion.10
  146.0 0.6 scatter_fusion.6
  146.6 0.6 scatter_fusion.11
  147.3 0.6 scatter_fusion.7
  148.5 8.9 %while.40 = (s32[]{:T(128)}, f32[4,8]{1,0:T(4,128)S(1)}, s32[]{:T(128)}, s32[]{:T(128)}, s32[]{:T(128)}, /*index=5*/s32[]{:T(128)}) while((s32[]{:T(128)}, f32[4,8]{1,0:T(4,128)S(1)}, s32[]{:T(128)}, s32[]{:T(128)}, s32[]{:T(128)}, /*index=5*/s32[]{:T(128)}) %tuple.117), condition=%wide.region_11.12_spmd, body=%wide.region_10.11_spmd.sunk | while | flops 84 | bytes 665 | solution.py:62
  148.5 0.6 dynamic_slice.112
  149.1 0.6 dynamic-slice_divide_fusion.7
  149.7 0.6 fusion.88
  150.7 0.6 dynamic_slice.112
  151.3 0.6 dynamic-slice_divide_fusion.7
  151.9 0.6 fusion.88
  152.9 0.6 dynamic_slice.112
  153.5 0.6 dynamic-slice_divide_fusion.7
  154.1 0.6 fusion.88
  155.1 0.6 dynamic_slice.112
  155.7 0.6 dynamic-slice_divide_fusion.7
  156.3 0.6 fusion.88
  157.4 75.2 %all-to-all-done = f32[4,32,64,256]{3,2,1,0:T(8,128)} async-done(((f32[4,32,64,256]{3,2,1,0:T(8,128)}), f32[4,32,64,256]{3,2,1,0:T(8,128)}, u32[]{:S(2)}, u32[]{:S(2)}) %all-to-all-start) | async-done | bytes 8388640 | tf_op jit(solution)/shard_map/all_to_all | solution.py:136
  232.6 4.0 copy.152
  236.6 8.6 %fusion.25 = f32[32,2,128,256]{3,2,0,1:T(8,128)S(1)} fusion(f32[32,2,128,256]{3,2,1,0:T(8,128)S(1)} %bitcast.137, f32[2,128,128]{2,1,0:T(8,128)S(1)} %copy-done.3), kind=kOutput, calls=%fused_computation.58 | convolution fusion | flops 3221225472 | bytes 16908288 | tf_op jit(solution)/shard_map/cij,ucjv->uciv/dot_general | solution.py:95
  245.2 3.4 copy-done.1
  249.6 5.4 multiply_add_fusion.1
  255.0 1.0 copy.158
  256.0 8.7 %copy.159 = f32[32,256,256]{2,0,1:T(8,128)} copy(f32[32,256,256]{2,1,0:T(8,128)S(1)} %bitcast.138) | data formatting | bytes 16777216 | tf_op jit(solution)/shard_map/reshape | solution.py:129
  264.7 8.7 %all-to-all-start.1 = ((f32[32,256,256]{2,0,1:T(8,128)}), f32[32,256,256]{2,0,1:T(8,128)}, u32[]{:S(2)}, u32[]{:S(2)}) async-start(f32[32,256,256]{2,0,1:T(8,128)} %copy.159), calls=%async_computation.1 | async-start | bytes 16777216 | tf_op jit(solution)/shard_map/all_to_all | solution.py:168
  273.3 8.1 %while.41 = (s32[]{:T(128)}, f32[4,8]{1,0:T(4,128)S(1)}, s32[]{:T(128)}, s32[]{:T(128)}, s32[]{:T(128)}, /*index=5*/s32[]{:T(128)}) while((s32[]{:T(128)}, f32[4,8]{1,0:T(4,128)S(1)}, s32[]{:T(128)}, s32[]{:T(128)}, s32[]{:T(128)}, /*index=5*/s32[]{:T(128)}) %tuple.120), condition=%wide.region_17.18_spmd, body=%wide.region_16.17_spmd.sunk | while | flops 84 | bytes 665 | solution.py:62
  281.9 175.4 %all-to-all-done.1 = f32[32,256,256]{2,0,1:T(8,128)} async-done(((f32[32,256,256]{2,0,1:T(8,128)}), f32[32,256,256]{2,0,1:T(8,128)}, u32[]{:S(2)}, u32[]{:S(2)}) %all-to-all-start.1) | async-done | bytes 8388640 | tf_op jit(solution)/shard_map/all_to_all | solution.py:168
  457.3 8.2 %copy.161 = f32[8,32,32,256]{3,2,1,0:T(8,128)S(1)} copy(f32[8,32,32,256]{3,1,2,0:T(8,128)} %bitcast.42) | data formatting | bytes 16777216 | tf_op jit(solution)/shard_map/all_to_all | solution.py:168
  465.5 13.4 %fusion.28 = f32[2,128,32,256]{3,1,2,0:T(8,128)S(1)} fusion(f32[2,128,32,256]{3,2,1,0:T(8,128)S(1)} %bitcast.139, f32[2,128,128]{2,1,0:T(8,128)S(1)} %copy-done.4), kind=kOutput, calls=%fused_computation.59 | convolution fusion | flops 3221225472 | bytes 16908288 | tf_op jit(solution)/shard_map/cij,cjuv->ciuv/dot_general | solution.py:95
  479.8 2.3 multiply_add_fusion
  482.1 5.1 copy.167
  487.1 186.4 %all_to_all.56 = f32[256,32,256]{2,1,0:T(8,128)S(1)} all-to-all(f32[256,32,256]{2,1,0:T(8,128)S(1)} %bitcast.140), channel_id=1, replica_groups=mesh['row'=4,'col'=8] {'col'}, dimensions={0} | all-to-all | bytes 16777216 | tf_op jit(solution)/shard_map/all_to_all | solution.py:171
  673.6 1.7 copy.168
  675.2 4.9 copy.169
  680.1 96.7 %all_to_all.57 = f32[32,256,256]{2,0,1:T(8,128)} all-to-all(f32[32,256,256]{2,0,1:T(8,128)S(1)} %copy.169), channel_id=1, replica_groups=mesh['row'=4,'col'=8] {'row'}, dimensions={1} | all-to-all | bytes 16777216 | tf_op jit(solution)/shard_map/all_to_all | solution.py:170
  776.8 12.2 %copy.171 = f32[32,64,4,256]{3,2,1,0:T(4,128)} copy(f32[32,64,4,256]{3,0,1,2:T(8,128)} %bitcast.143) | data formatting | bytes 16777216 | tf_op jit(solution)/shard_map/all_to_all | solution.py:170
  789.0 10.7 %all_to_all.51 = f32[32,64,1024]{2,1,0:T(8,128)} reshape(f32[32,64,4,256]{3,2,1,0:T(4,128)} %copy.171) | data formatting | bytes 16777216 | tf_op jit(solution)/shard_map/all_to_all | solution.py:170
  799.7 12.1 %add.391 = f32[32,64,1024]{2,1,0:T(8,128)} add(f32[32,64,1024]{2,1,0:T(8,128)} %param.14, f32[32,64,1024]{2,1,0:T(8,128)} %all_to_all.51) | non-fusion elementwise | flops 2097152 | bytes 25165824 | tf_op jit(solution)/shard_map/add | solution.py:177
  (230 shorter events, 47.7 us)
Async XLA Ops:
  1.8 57.2 %collective-permute-start = (f32[32,1,1024]{2,0,1:T(8,128)S(1)}, f32[32,1,1024]{2,0,1:T(8,128)S(1)}, u32[]{:S(2)}, u32[]{:S(2)}) collective-permute-start(f32[32,1,1024]{2,0,1:T(8,128)S(1)} %copy.181), channel_id=1, source_target_pairs={{8,0},{16,8},{24,16},{9,1},{17,9},{25,17},{10,2},{18,10},{26,18},{... | collective-permute-start | bytes 393224 | tf_op jit(solution)/shard_map/ppermute | solution.py:18
  3.1 56.0 %collective-permute-start.1 = (f32[32,1,1024]{2,0,1:T(8,128)S(1)}, f32[32,1,1024]{2,0,1:T(8,128)S(1)}, u32[]{:S(2)}, u32[]{:S(2)}) collective-permute-start(f32[32,1,1024]{2,0,1:T(8,128)S(1)} %copy.182), channel_id=1, source_target_pairs={{0,8},{8,16},{16,24},{1,9},{9,17},{17,25},{2,10},{10,18},{18,26},{... | collective-permute-start | bytes 393224 | tf_op jit(solution)/shard_map/ppermute | solution.py:17
  8.7 13.4 %copy-start.2 = (f32[8,128,128]{2,1,0:T(8,128)S(1)}, f32[8,128,128]{2,1,0:T(8,128)}, u32[]{:S(2)}) copy-start(f32[8,128,128]{2,1,0:T(8,128)} %param.19) | copy-start | bytes 1572868
  8.7 13.8 %copy-start.5 = (f32[1024]{0:T(1024)S(1)}, f32[1024]{0:T(1024)}, u32[]{:S(2)}) copy-start(f32[1024]{0:T(1024)} %param.16) | copy-start | bytes 12292
  8.7 50.1 %copy-start.6 = (f32[256]{0:T(256)S(1)}, f32[256]{0:T(256)}, u32[]{:S(2)}) copy-start(f32[256]{0:T(256)} %param.18) | copy-start | bytes 3076
  8.7 50.1 %copy-start.7 = (f32[256]{0:T(256)S(1)}, f32[256]{0:T(256)}, u32[]{:S(2)}) copy-start(f32[256]{0:T(256)} %param.17) | copy-start | bytes 3076
  60.4 5.5 collective-permute-start.2
  61.7 4.2 collective-permute-start.3
  94.4 8.4 %copy-start = (f32[32,64,8,128]{3,1,0,2:T(8,128)}, f32[32,64,8,128]{3,1,0,2:T(8,128)S(1)}, u32[]{:S(2)}) copy-start(f32[32,64,8,128]{3,1,0,2:T(8,128)S(1)} %fusion.22) | copy-start | bytes 25165828
  134.0 8.1 copy-start.4
  134.0 9.0 %copy-start.3 = (f32[2,128,128]{2,1,0:T(8,128)S(1)}, f32[2,128,128]{2,1,0:T(8,128)}, u32[]{:S(2)}) copy-start(f32[2,128,128]{2,1,0:T(8,128)} %param.20) | copy-start | bytes 393220
  134.0 98.6 %all-to-all-start = ((f32[4,32,64,256]{3,2,1,0:T(8,128)}), f32[4,32,64,256]{3,2,1,0:T(8,128)}, u32[]{:S(2)}, u32[]{:S(2)}) async-start(f32[4,32,64,256]{3,2,1,0:T(8,128)} %pad_maximum_fusion.9), calls=%async_computation | async-start | bytes 16777216 | tf_op jit(solution)/shard_map/all_to_all | solution.py:136
  245.2 3.4 copy-start.1
  264.7 192.6 %all-to-all-start.1 = ((f32[32,256,256]{2,0,1:T(8,128)}), f32[32,256,256]{2,0,1:T(8,128)}, u32[]{:S(2)}, u32[]{:S(2)}) async-start(f32[32,256,256]{2,0,1:T(8,128)} %copy.159), calls=%async_computation.1 | async-start | bytes 16777216 | tf_op jit(solution)/shard_map/all_to_all | solution.py:168
